TPU v7x, 128 devices: a whole 4x4x4 slice. The times are simulated.
128 devices in a mesh: row: 8 (over x, core), col: 16 (over y, z).
Axes of the slice: x: 4, y: 4, z: 4, core: 2. Of those that a mesh axis runs over, the one named last changes fastest.
Arguments:
- imu: bfloat16 [32768, 128], P(('row', 'col')), may hold values from -30 to 30
- camera: bfloat16 [16, 2048, 128], P('col', 'row'), may hold values from -30 to 30
- imu_mass: float32 [32768], P('row'), may hold values from 0.3 to 3
- cam_mass: float32 [32768], P('col'), may hold values from 0.3 to 3
Outputs:
- grad_imu: float32 [32768, 128], P(('row', 'col'))
- grad_camera: float32 [16, 2048, 128], P('col', 'row')
All inputs are finite; a program needn't handle non-finite values.
Results may differ from a plain program's by a relative error of at most 0.0028.
Values may be sent and summed in bfloat16 or wider, within the bound.
A program may use at most 128 MiB of HBM per device.

v0:
```python
import math
import jax
import jax.numpy as jnp
from jax import lax
from jax.sharding import PartitionSpec as P

D = 128
ITERS = 3


def cost_block(rows, rows_sq, cols, cols_sq):
    cross = jnp.dot(rows, cols.T, preferred_element_type=jnp.float32)
    return rows_sq[:, None] + cols_sq[None, :] - 2.0 * cross


def squares(values):
    return jnp.sum(jnp.square(values.astype(jnp.float32)), axis=1)


def combine(part, axis):
    parts = lax.all_gather(part, axis, axis=0)
    top = jnp.max(parts, axis=0)
    return top + jnp.log(jnp.sum(jnp.exp(parts - top[None, :]), axis=0))


def local(imu, camera, imu_mass, cam_mass):
    epsilon = D / 20.0
    imu_rows = lax.all_gather(imu, "col", axis=0, tiled=True)
    cam_rows = lax.all_gather(camera, "row", axis=1, tiled=True)[0]
    rows = imu_rows.shape[0]
    cols = cam_rows.shape[0]
    block = math.gcd(rows, 512)
    count = rows // block
    rows_sq = squares(imu_rows)
    cols_sq = squares(cam_rows)
    log_a = jnp.log(imu_mass)
    log_b = jnp.log(cam_mass)
    stored = cost_block(imu_rows, rows_sq, cam_rows, cols_sq)

    def tile(k):
        return lax.dynamic_slice_in_dim(stored, k * block, block, 0)

    blocks = jnp.arange(count, dtype=jnp.int32)

    def row_lse(g):

        def single(k):
            scores = (g[None, :] - tile(k)) / epsilon
            peak = jnp.max(scores, axis=1)
            return (peak, jnp.sum(jnp.exp(scores - peak[:, None]), axis=1))

        peak, total = lax.map(single, blocks)
        peak = peak.reshape(rows)
        total = total.reshape(rows)
        return combine(peak + jnp.log(total), "col")

    def col_lse(f):

        def advance(k, carry):
            peak, total = carry
            f_blk = lax.dynamic_slice_in_dim(f, k * block, block, 0)
            scores = (f_blk[:, None] - tile(k)) / epsilon
            new_peak = jnp.maximum(peak, jnp.max(scores, axis=0))
            total = total * jnp.exp(peak - new_peak) + jnp.sum(
                jnp.exp(scores - new_peak[None, :]), axis=0
            )
            return (new_peak, total)

        start = (jnp.full((cols,), -1e30, jnp.float32), jnp.zeros((cols,), jnp.float32))
        peak, total = lax.fori_loop(0, count, advance, start)
        return combine(peak + jnp.log(total), "row")

    g = jnp.zeros((cols,), jnp.float32)
    f = jnp.zeros((rows,), jnp.float32)
    for step in range(ITERS):
        f = epsilon * log_a - epsilon * row_lse(g)
        g = epsilon * log_b - epsilon * col_lse(f)

    def plan_rows(k):
        f_blk = lax.dynamic_slice_in_dim(f, k * block, block, 0)
        return jnp.exp((f_blk[:, None] + g[None, :] - tile(k)) / epsilon).astype(jnp.bfloat16)

    plan = lax.map(plan_rows, blocks).reshape(rows, cols)
    row_total = jnp.sum(plan, axis=1, dtype=jnp.float32)
    col_total = jnp.sum(plan, axis=0, dtype=jnp.float32)
    imu_share = rows // lax.axis_size("col")
    cam_share = cols // lax.axis_size("row")
    plan_part = plan
    own = imu_rows.astype(jnp.float32)
    weight = row_total
    pulled = jnp.dot(plan_part, cam_rows, preferred_element_type=jnp.float32)
    grad_imu = lax.psum_scatter(
        2.0 * (weight[:, None] * own - pulled), "col", scatter_dimension=0, tiled=True
    )
    plan_part = plan
    own = cam_rows.astype(jnp.float32)
    weight = col_total
    pulled = lax.dot_general(
        plan_part, imu_rows, (((0,), (0,)), ((), ())), preferred_element_type=jnp.float32
    )
    grad_cam = lax.psum_scatter(
        2.0 * (weight[:, None] * own - pulled), "row", scatter_dimension=0, tiled=True
    )
    return (grad_imu, grad_cam[None])


def solution(mesh):
    in_specs = (P(("row", "col"), None), P("col", "row", None), P("row"), P("col"))
    out_specs = (P(("row", "col"), None), P("col", "row", None))
    return jax.shard_map(local, mesh=mesh, in_specs=in_specs, out_specs=out_specs, check_vma=False)
```

profile of v0, /device:TPU:0, one launch (start us, length us, event | category | flops | bytes accessed | tf_op | source)
XLA Modules:
  0.0 668.9 jit_solution(3283846206429722116)
XLA Ops:
  8.0 13.8 %all_gather.37 = bf16[1,2048,128]{2,1,0:T(8,128)(2,1)S(1)} all-gather(bf16[1,256,128]{2,1,0:T(8,128)(2,1)} %param.19), channel_id=1, replica_groups=mesh['row'=8,'col'=16] {'row'}, dimensions={1}, use_global_device_ids=true | all-gather | bytes 589824 | tf_op jit(solution)/shard_map/all_gather | solution.py:29
  22.1 33.4 %all-gather.8.cloned.1.call-done = bf16[4096,128]{1,0:T(8,128)(2,1)} async-done(((bf16[256,128]{1,0:T(8,128)(2,1)}), bf16[4096,128]{1,0:T(8,128)(2,1)}) %all-gather.8.cloned.1.call-update) | async-done | bytes 1048592 | tf_op jit(solution)/shard_map/all_gather | solution.py:28
  57.4 14.3 %multiply_subtract_fusion = f32[4096,2048]{1,0:T(8,128)} fusion(f32[2048]{0:T(1024)S(1)} %fusion.14, f32[4096]{0:T(1024)S(1)} %fusion.13, bf16[4096,128]{1,0:T(8,128)(2,1)} %all-gather.8.cloned.1.call-done, bf16[1,2048,128]{2,1,0:T(8,128)(2,1)S(1)} %all_gather.37), kind=kOutput, calls=%fused_computation.32 | convolution fusion | flops 2172649472 | bytes 35151872 | tf_op jit(solution)/shard_map/dot_general | solution.py:12
  71.7 56.4 %while.94 = (s32[]{:T(128)}, f32[8,512]{1,0:T(8,128)S(1)}, f32[8,512]{1,0:T(8,128)S(1)}, s32[8]{0:T(128)S(1)}, f32[4096,2048]{1,0:T(8,128)}, /*index=5*/s32[]{:T(128)}, s32[1]{0:T(128)}, s32[]{:T(128)}, s32[]{:T(128)}) while((s32[]{:T(128)}, f32[8,512]{1,0:T(8,128)S(1)}, f32[8,512]{1,0:T(8,128)S(1)}, s32[8]{0:T(128)S(1)}, ...), condition=%wide.region_5.6_spmd, body=%wide.region_2.5_spmd.sunk | while | flops 7339014 | bytes 8403111 | solution.py:52
  128.2 23.1 %all-gather.3 = f32[16,1,4096]{2,1,0:T(1,128)S(1)} all-gather(f32[1,1,4096]{2,1,0:T(1,128)S(1)} %reshape.116), channel_id=1, replica_groups=mesh['row'=8,'col'=16] {'col'}, dimensions={0}, use_global_device_ids=true | all-gather | bytes 278528 | tf_op jit(solution)/shard_map/all_gather | solution.py:21
  151.7 47.5 %while.98 = (s32[]{:T(128)}, f32[2048]{0:T(1024)S(1)}, f32[2048]{0:T(1024)S(1)}, f32[4096]{0:T(1024)S(1)}, f32[4096,2048]{1,0:T(8,128)}, /*index=5*/s32[]{:T(128)}, s32[]{:T(128)}, s32[]{:T(128)}, s32[]{:T(128)}) while((s32[]{:T(128)}, f32[2048]{0:T(1024)S(1)}, f32[2048]{0:T(1024)S(1)}, f32[4096]{0:T(1024)S(1)}, ...), condition=%wide.region_11.12_spmd.clone, body=%wide.region_8.11_spmd.clone.sunk | while | flops 7350279 | bytes 8503458 | solution.py:70
  199.2 13.1 %all-gather = f32[16384]{0:T(1024)S(1)} all-gather(f32[2048]{0:T(1024)S(1)} %log_add_fusion.5), channel_id=2, replica_groups=mesh['row'=8,'col'=16] {'row'}, dimensions={0}, use_global_device_ids=true | all-gather | bytes 73728 | tf_op jit(solution)/shard_map/all_gather | solution.py:21
  212.4 57.6 %while.95 = (s32[]{:T(128)}, f32[8,512]{1,0:T(8,128)S(1)}, f32[8,512]{1,0:T(8,128)S(1)}, f32[2048]{0:T(1024)S(1)}, s32[8]{0:T(128)S(1)}, /*index=5*/f32[4096,204...) while((s32[]{:T(128)}, f32[8,512]{1,0:T(8,128)S(1)}, f32[8,512]{1,0:T(8,128)S(1)}, ...), condition=%wide.region_17.18_spmd, body=%wide.region_14.17_spmd.sunk | while | flops 7339014 | bytes 8419503 | solution.py:52
  266.7 3.1 exponential_reduce_fusion.16
  270.0 21.7 %all-gather.4 = f32[16,1,4096]{2,1,0:T(1,128)S(1)} all-gather(f32[1,1,4096]{2,1,0:T(1,128)S(1)} %reshape.118), channel_id=1, replica_groups=mesh['row'=8,'col'=16] {'col'}, dimensions={0}, use_global_device_ids=true | all-gather | bytes 278528 | tf_op jit(solution)/shard_map/all_gather | solution.py:21
  292.2 47.5 %while.99 = (s32[]{:T(128)}, f32[2048]{0:T(1024)S(1)}, f32[2048]{0:T(1024)S(1)}, f32[4096]{0:T(1024)S(1)}, f32[4096,2048]{1,0:T(8,128)}, /*index=5*/s32[]{:T(128)}, s32[]{:T(128)}, s32[]{:T(128)}, s32[]{:T(128)}) while((s32[]{:T(128)}, f32[2048]{0:T(1024)S(1)}, f32[2048]{0:T(1024)S(1)}, f32[4096]{0:T(1024)S(1)}, ...), condition=%wide.region_23.24_spmd.clone, body=%wide.region_20.23_spmd.clone.sunk | while | flops 7350279 | bytes 8503458 | solution.py:70
  339.7 12.8 %all-gather.1 = f32[16384]{0:T(1024)S(1)} all-gather(f32[2048]{0:T(1024)S(1)} %log_add_fusion.4), channel_id=3, replica_groups=mesh['row'=8,'col'=16] {'row'}, dimensions={0}, use_global_device_ids=true | all-gather | bytes 73728 | tf_op jit(solution)/shard_map/all_gather | solution.py:21
  352.6 56.7 %while.96 = (s32[]{:T(128)}, f32[8,512]{1,0:T(8,128)S(1)}, f32[8,512]{1,0:T(8,128)S(1)}, f32[2048]{0:T(1024)S(1)}, s32[8]{0:T(128)S(1)}, /*index=5*/f32[4096,204...) while((s32[]{:T(128)}, f32[8,512]{1,0:T(8,128)S(1)}, f32[8,512]{1,0:T(8,128)S(1)}, ...), condition=%wide.region_29.30_spmd, body=%wide.region_26.29_spmd.sunk | while | flops 7339014 | bytes 8419503 | solution.py:52
  363.5 3.1 exponential_reduce_fusion.17
  377.6 3.1 exponential_reduce_fusion.17
  409.3 23.1 %all-gather.5 = f32[16,1,4096]{2,1,0:T(1,128)S(1)} all-gather(f32[1,1,4096]{2,1,0:T(1,128)S(1)} %reshape.120), channel_id=1, replica_groups=mesh['row'=8,'col'=16] {'col'}, dimensions={0}, use_global_device_ids=true | all-gather | bytes 278528 | tf_op jit(solution)/shard_map/all_gather | solution.py:21
  432.8 47.5 %while.100 = (s32[]{:T(128)}, f32[2048]{0:T(1024)S(1)}, f32[2048]{0:T(1024)S(1)}, f32[4096]{0:T(1024)S(1)}, f32[4096,2048]{1,0:T(8,128)}, /*index=5*/s32[]{:T(128)}, s32[]{:T(128)}, s32[]{:T(128)}, s32[]{:T(128)}) while((s32[]{:T(128)}, f32[2048]{0:T(1024)S(1)}, f32[2048]{0:T(1024)S(1)}, f32[4096]{0:T(1024)S(1)}, ...), condition=%wide.region_35.36_spmd.clone, body=%wide.region_32.35_spmd.clone.sunk | while | flops 7350279 | bytes 8503458 | solution.py:70
  480.3 13.0 %all-gather.2 = f32[16384]{0:T(1024)S(1)} all-gather(f32[2048]{0:T(1024)S(1)} %log_add_fusion.3), channel_id=4, replica_groups=mesh['row'=8,'col'=16] {'row'}, dimensions={0}, use_global_device_ids=true | all-gather | bytes 73728 | tf_op jit(solution)/shard_map/all_gather | solution.py:21
  493.4 45.2 %while.97 = (s32[]{:T(128)}, bf16[8,512,2048]{2,1,0:T(8,128)(2,1)}, s32[8]{0:T(128)S(1)}, f32[4096]{0:T(1024)S(1)}, f32[2048]{0:T(1024)S(1)}, /*index=5*/f32[409...) while((s32[]{:T(128)}, bf16[8,512,2048]{2,1,0:T(8,128)(2,1)}, s32[8]{0:T(128)S(1)}, ...), condition=%wide.region_39.40_spmd, body=%wide.region_38.39_spmd.sunk | while | flops 4194310 | bytes 6306471 | solution.py:83
  494.7 4.3 fusion.40
  500.3 4.4 fusion.40
  506.0 4.3 fusion.40
  511.6 4.3 fusion.40
  517.3 4.4 fusion.40
  522.9 4.3 fusion.40
  528.5 4.4 fusion.40
  534.2 4.3 fusion.40
  538.5 8.5 %convert_reduce_fusion = (f32[2048]{0:T(1024)S(1)}, f32[8,512]{1,0:T(8,128)S(1)}) fusion(bf16[8,512,2048]{2,1,0:T(8,128)(2,1)} %get-tuple-element.425), kind=kLoop, calls=%fused_computation.30 | loop fusion | flops 25159680 | bytes 16801792 | tf_op jit(solution)/shard_map/reduce_sum | solution.py:85
  549.2 6.0 fusion.12
  555.3 11.7 %fusion.11 = f32[4096,128]{1,0:T(8,128)} fusion(bf16[4096,2048]{1,0:T(8,128)(2,1)} %bitcast.69, bf16[4096,128]{1,0:T(8,128)(2,1)S(1)} %copy-done.1, f32[4096]{0:T(1024)S(1)} %bitcast.78, bf16[1,2048,128]{2,1,0:T(8,128)(2,1)S(1)} %all_gather.37), kind=kOutput, calls=%fused_computation.34 | convolution fusion | flops 2149580800 | bytes 20463616 | tf_op jit(solution)/shard_map/dot_general | solution.py:91
  567.0 18.1 %reduce-scatter.5.cloned.1.call-done = f32[256,128]{1,0:T(8,128)} async-done(((f32[2048,128]{1,0:T(8,128)}), f32[256,128]{1,0:T(8,128)}) %reduce-scatter.5.cloned.1.call-update) | async-done | bytes 131088 | tf_op jit(solution)/shard_map/reduce_scatter | solution.py:101
  585.1 77.2 %reduce-scatter.3.cloned.1.call-done = f32[256,128]{1,0:T(8,128)} async-done(((f32[4096,128]{1,0:T(8,128)}), f32[256,128]{1,0:T(8,128)}) %reduce-scatter.3.cloned.1.call-update) | async-done | bytes 131088 | tf_op jit(solution)/shard_map/reduce_scatter | solution.py:92
  (341 shorter events, 299.4 us)
Async XLA Ops:
  7.2 48.4 %all-gather.8.cloned.1.call-start = ((), (), s32[]{:S(2)}) async-start(), calls=%async_computation.2 | async-start | bytes 1114112 | tf_op jit(solution)/shard_map/all_gather | solution.py:28
  7.9 577.2 %reduce-scatter.5.cloned.1.call-start = ((), (), s32[]{:S(2)}) async-start(), calls=%async_computation.4 | async-start | bytes 1179648 | tf_op jit(solution)/shard_map/reduce_scatter | solution.py:101
  71.7 80.0 %copy-start.2 = (f32[4096]{0:T(1024)S(1)}, f32[4096]{0:T(1024)}, u32[]{:S(2)}) copy-start(f32[4096]{0:T(1024)} %param.20) | copy-start | bytes 49156
  151.7 60.7 %copy-start.3 = (f32[2048]{0:T(1024)S(1)}, f32[2048]{0:T(1024)}, u32[]{:S(2)}) copy-start(f32[2048]{0:T(1024)} %param.21) | copy-start | bytes 24580
  493.3 53.7 %copy-start.1 = (bf16[4096,128]{1,0:T(8,128)(2,1)S(1)}, bf16[4096,128]{1,0:T(8,128)(2,1)}, u32[]{:S(2)}) copy-start(bf16[4096,128]{1,0:T(8,128)(2,1)} %all-gather.8.cloned.1.call-done) | copy-start | bytes 3145732
  538.5 10.7 %copy-start = (bf16[8,512,2048]{2,1,0:T(8,128)(2,1)S(1)}, bf16[8,512,2048]{2,1,0:T(8,128)(2,1)}, u32[]{:S(2)}) copy-start(bf16[8,512,2048]{2,1,0:T(8,128)(2,1)} %get-tuple-element.425) | copy-start | bytes 50331652
  555.3 107.1 %reduce-scatter.3.cloned.1.call-start = ((), (), s32[]{:S(2)}) async-start(), calls=%async_computation.3 | async-start | bytes 2228224 | tf_op jit(solution)/shard_map/reduce_scatter | solution.py:92
Sparse Core Ops, SparseCore 0:
  10.1 45.3 all-gather.7
  555.4 29.6 reduce-scatter.4
  588.9 73.3 reduce-scatter.2
where the time goes:
time: 673 us; the launch traced here: 669 us
  other arithmetic  325 us (48%)
  waiting for transfers between devices  129 us (19%)
  blocking collectives  120 us (18%)
  matrix products  32 us (5%)
  local copies, waits for them, and re-layouts  26.3 us (4%)
  loops' own time  21.8 us (3%)
  between operations  14.2 us (2%)
    all_gather x6, blocking collectives, combine(): parts = lax.all_gather(part, axis, axis=0)  107 us
    reduce_scatter x1, waiting for transfers between devices, local(): lax.psum_scatter(2.0 * (weight[:, None] * own - pulled), 'col', scatter_d...  77.2 us
    reduce_sum x24, other arithmetic, single(): return (peak, jnp.sum(jnp.exp(scores - peak[:, None]), axis=1))  74.8 us
    reduce_sum x24, other arithmetic, advance(): jnp.sum(jnp.exp(scores - new_peak[None, :]), axis=0)  74.4 us
    reduce_max x24, other arithmetic, single(): peak = jnp.max(scores, axis=1)  64.3 us
    reduce_max x24, other arithmetic, advance(): new_peak = jnp.maximum(peak, jnp.max(scores, axis=0))  64.1 us
    dynamic_update_slice x8, other arithmetic, local(): plan = lax.map(plan_rows, blocks).reshape(rows, cols)  34.6 us
    all_gather x1, waiting for transfers between devices, local(): imu_rows = lax.all_gather(imu, 'col', axis=0, tiled=True)  33.4 us
  transfers between devices with their start and end apart: 3, of which 3 were waited for; matrix products, arithmetic and copies ran while one was open for 2% of the time, Pallas kernels for 0%

commit v1 on v0

--- a/solution.py
+++ b/solution.py
@@ -1,3 +1,4 @@
+import functools
 import math
 import jax
 import jax.numpy as jnp
@@ -6,6 +7,33 @@
 
 D = 128
 ITERS = 3
+
+
+def switch_the_desk(obj, dev_axis, d_out):
+    lower, step_out, formed = (lax.axis_size(dev_axis), lax.axis_index(dev_axis), obj.shape[d_out])
+    block_last = lax.dynamic_update_slice_in_dim(
+        jnp.zeros(
+            [dev_i * lower if d == d_out else dev_i for d, dev_i in enumerate(obj.shape)], obj.dtype
+        ),
+        obj,
+        step_out * formed,
+        axis=d_out,
+    )
+    known = before = obj
+    for w in range(1, lower // 2 + 1):
+        known = lax.ppermute(known, dev_axis, [(d, (d + 1) % lower) for d in range(lower)])
+        block_last = lax.dynamic_update_slice_in_dim(
+            block_last, known, (step_out - w) % lower * formed, axis=d_out
+        )
+        if 2 * w < lower:
+            before = lax.ppermute(before, dev_axis, [(d, (d - 1) % lower) for d in range(lower)])
+            block_last = lax.dynamic_update_slice_in_dim(
+                block_last, before, (step_out + w) % lower * formed, axis=d_out
+            )
+    return block_last
+
+
+list_the_core = functools.partial(switch_the_desk, dev_axis="row", d_out=1)
 
 
 def cost_block(rows, rows_sq, cols, cols_sq):
@@ -26,7 +54,7 @@
 def local(imu, camera, imu_mass, cam_mass):
     epsilon = D / 20.0
     imu_rows = lax.all_gather(imu, "col", axis=0, tiled=True)
-    cam_rows = lax.all_gather(camera, "row", axis=1, tiled=True)[0]
+    cam_rows = list_the_core(camera)[0]
     rows = imu_rows.shape[0]
     cols = cam_rows.shape[0]
     block = math.gcd(rows, 512)

time: 673 us -> 711 us (1.056)
  local copies, waits for them, and re-layouts: 26.3 us -> 62.4 us
  blocking collectives: 120 us -> 107 us
  starting transfers between devices: 0.12 us -> 8.93 us
    while x24 -> x25, local copies, waits for them, and re-layouts: 0.06 us -> 33.4 us  [the longest x1 33.3 us: row_lse(): peak, total = lax.map(single, blocks)]
    all_gather x1 -> x0, blocking collectives: 13.8 us -> none  [local(): cam_rows = lax.all_gather(camera, 'row', axis=1, tiled=True)[0]]
    ppermute x0 -> x7, waiting for transfers between devices: none -> 9.65 us  [the longest x4 9.58 us: switch_the_desk(): lax.ppermute(known, dev_axis, [(d, (d + 1) % lower) for d in range(lower)])]
    ppermute x0 -> x7, starting transfers between devices: none -> 8.82 us  [the longest x3 8.79 us: switch_the_desk(): lax.ppermute(before, dev_axis, [(d, (d - 1) % lower) for d in range(lower)])]
  transfers between devices with their start and end apart: 3 -> 10, of which waited for: 3 -> 8; matrix products, arithmetic and copies ran while one was open for 2% -> 2% of each run, Pallas kernels for 0% -> 0%
where the time goes in v1:
time: 711 us; the launch traced here: 706 us
  other arithmetic  325 us (46%)
  waiting for transfers between devices  133 us (19%)
  blocking collectives  107 us (15%)
  local copies, waits for them, and re-layouts  62.4 us (9%)
  matrix products  32 us (5%)
  loops' own time  24 us (3%)
  between operations  14.4 us (2%)
  starting transfers between devices  8.93 us (1%)
    all_gather x6, blocking collectives, combine(): parts = lax.all_gather(part, axis, axis=0)  107 us
    reduce_scatter x1, waiting for transfers between devices, local(): lax.psum_scatter(2.0 * (weight[:, None] * own - pulled), 'col', scatter_d...  77.2 us
    reduce_sum x24, other arithmetic, single(): return (peak, jnp.sum(jnp.exp(scores - peak[:, None]), axis=1))  74.8 us
    reduce_sum x24, other arithmetic, advance(): jnp.sum(jnp.exp(scores - new_peak[None, :]), axis=0)  74.4 us
    reduce_max x24, other arithmetic, single(): peak = jnp.max(scores, axis=1)  64.3 us
    reduce_max x24, other arithmetic, advance(): new_peak = jnp.maximum(peak, jnp.max(scores, axis=0))  64.1 us
    dynamic_update_slice x8, other arithmetic, local(): plan = lax.map(plan_rows, blocks).reshape(rows, cols)  34.7 us
    while x1, local copies, waits for them, and re-layouts, row_lse(): peak, total = lax.map(single, blocks)  33.3 us
  transfers between devices with their start and end apart: 10, of which 8 were waited for; matrix products, arithmetic and copies ran while one was open for 2% of the time, Pallas kernels for 0%

profile of v1, /device:TPU:0, one launch (start us, length us, event | category | flops | bytes accessed | tf_op | source)
XLA Modules:
  0.0 706.2 jit_solution(15811998476709621810)
XLA Ops:
  22.2 4.9 collective-permute-done.6
  27.4 28.1 %all-gather.8.cloned.1.call-done = bf16[4096,128]{1,0:T(8,128)(2,1)} async-done(((bf16[256,128]{1,0:T(8,128)(2,1)}), bf16[4096,128]{1,0:T(8,128)(2,1)}) %all-gather.8.cloned.1.call-update) | async-done | bytes 1048592 | tf_op jit(solution)/shard_map/all_gather | solution.py:56
  57.4 14.3 %bitcast_subtract_fusion = f32[4096,2048]{0,1:T(8,128)} fusion(f32[2048]{0:T(1024)S(1)} %fusion.13, f32[4096]{0:T(1024)S(1)} %fusion.12, bf16[2048,128]{1,0:T(8,128)(2,1)S(1)} %bitcast_dynamic-update-slice_fusion, bf16[4096,128]{1,0:T(8,128)(2,1)} %all-gather.8.cloned.1.call-done), kind=kOutput, calls=%fused_computation.32 | convolution fusion | flops 2172649472 | bytes 35151872 | tf_op jit(solution)/shard_map/dot_general | solution.py:40
  71.7 33.3 %copy.20 = f32[4096,2048]{1,0:T(8,128)} copy(f32[4096,2048]{0,1:T(8,128)} %bitcast_subtract_fusion) | data formatting | bytes 67108864 | tf_op jit(solution)/shard_map/while | solution.py:80
  105.0 58.2 %while.94 = (s32[]{:T(128)}, f32[8,512]{1,0:T(8,128)S(1)}, f32[8,512]{1,0:T(8,128)S(1)}, s32[8]{0:T(128)S(1)}, f32[4096,2048]{1,0:T(8,128)}, /*index=5*/s32[]{:T(128)}, s32[1]{0:T(128)}, s32[]{:T(128)}, s32[]{:T(128)}) while((s32[]{:T(128)}, f32[8,512]{1,0:T(8,128)S(1)}, f32[8,512]{1,0:T(8,128)S(1)}, s32[8]{0:T(128)S(1)}, ...), condition=%wide.region_5.6_spmd, body=%wide.region_2.5_spmd.sunk | while | flops 7339014 | bytes 8403111 | solution.py:80
  163.3 23.1 %all-gather.3 = f32[16,1,4096]{2,1,0:T(1,128)S(1)} all-gather(f32[1,1,4096]{2,1,0:T(1,128)S(1)} %reshape.132), channel_id=1, replica_groups=mesh['row'=8,'col'=16] {'col'}, dimensions={0}, use_global_device_ids=true | all-gather | bytes 278528 | tf_op jit(solution)/shard_map/all_gather | solution.py:49
  186.8 47.5 %while.98 = (s32[]{:T(128)}, f32[2048]{0:T(1024)S(1)}, f32[2048]{0:T(1024)S(1)}, f32[4096]{0:T(1024)S(1)}, f32[4096,2048]{1,0:T(8,128)}, /*index=5*/s32[]{:T(128)}, s32[]{:T(128)}, s32[]{:T(128)}, s32[]{:T(128)}) while((s32[]{:T(128)}, f32[2048]{0:T(1024)S(1)}, f32[2048]{0:T(1024)S(1)}, f32[4096]{0:T(1024)S(1)}, ...), condition=%wide.region_11.12_spmd.clone, body=%wide.region_8.11_spmd.clone.sunk | while | flops 7350279 | bytes 8503458 | solution.py:98
  234.3 13.0 %all-gather = f32[16384]{0:T(1024)S(1)} all-gather(f32[2048]{0:T(1024)S(1)} %log_add_fusion.5), channel_id=2, replica_groups=mesh['row'=8,'col'=16] {'row'}, dimensions={0}, use_global_device_ids=true | all-gather | bytes 73728 | tf_op jit(solution)/shard_map/all_gather | solution.py:49
  247.5 58.3 %while.95 = (s32[]{:T(128)}, f32[8,512]{1,0:T(8,128)S(1)}, f32[8,512]{1,0:T(8,128)S(1)}, f32[2048]{0:T(1024)S(1)}, s32[8]{0:T(128)S(1)}, /*index=5*/f32[4096,204...) while((s32[]{:T(128)}, f32[8,512]{1,0:T(8,128)S(1)}, f32[8,512]{1,0:T(8,128)S(1)}, ...), condition=%wide.region_17.18_spmd, body=%wide.region_14.17_spmd.sunk | while | flops 7339014 | bytes 8419503 | solution.py:80
  305.8 21.7 %all-gather.4 = f32[16,1,4096]{2,1,0:T(1,128)S(1)} all-gather(f32[1,1,4096]{2,1,0:T(1,128)S(1)} %reshape.134), channel_id=1, replica_groups=mesh['row'=8,'col'=16] {'col'}, dimensions={0}, use_global_device_ids=true | all-gather | bytes 278528 | tf_op jit(solution)/shard_map/all_gather | solution.py:49
  327.9 47.5 %while.99 = (s32[]{:T(128)}, f32[2048]{0:T(1024)S(1)}, f32[2048]{0:T(1024)S(1)}, f32[4096]{0:T(1024)S(1)}, f32[4096,2048]{1,0:T(8,128)}, /*index=5*/s32[]{:T(128)}, s32[]{:T(128)}, s32[]{:T(128)}, s32[]{:T(128)}) while((s32[]{:T(128)}, f32[2048]{0:T(1024)S(1)}, f32[2048]{0:T(1024)S(1)}, f32[4096]{0:T(1024)S(1)}, ...), condition=%wide.region_23.24_spmd.clone, body=%wide.region_20.23_spmd.clone.sunk | while | flops 7350279 | bytes 8503458 | solution.py:98
  375.4 12.8 %all-gather.1 = f32[16384]{0:T(1024)S(1)} all-gather(f32[2048]{0:T(1024)S(1)} %log_add_fusion.4), channel_id=3, replica_groups=mesh['row'=8,'col'=16] {'row'}, dimensions={0}, use_global_device_ids=true | all-gather | bytes 73728 | tf_op jit(solution)/shard_map/all_gather | solution.py:49
  388.3 58.2 %while.96 = (s32[]{:T(128)}, f32[8,512]{1,0:T(8,128)S(1)}, f32[8,512]{1,0:T(8,128)S(1)}, f32[2048]{0:T(1024)S(1)}, s32[8]{0:T(128)S(1)}, /*index=5*/f32[4096,204...) while((s32[]{:T(128)}, f32[8,512]{1,0:T(8,128)S(1)}, f32[8,512]{1,0:T(8,128)S(1)}, ...), condition=%wide.region_29.30_spmd, body=%wide.region_26.29_spmd.sunk | while | flops 7339014 | bytes 8419503 | solution.py:80
  392.4 3.1 exponential_reduce_fusion.17
  414.2 3.1 exponential_reduce_fusion.17
  446.6 23.1 %all-gather.5 = f32[16,1,4096]{2,1,0:T(1,128)S(1)} all-gather(f32[1,1,4096]{2,1,0:T(1,128)S(1)} %reshape.136), channel_id=1, replica_groups=mesh['row'=8,'col'=16] {'col'}, dimensions={0}, use_global_device_ids=true | all-gather | bytes 278528 | tf_op jit(solution)/shard_map/all_gather | solution.py:49
  470.1 47.5 %while.100 = (s32[]{:T(128)}, f32[2048]{0:T(1024)S(1)}, f32[2048]{0:T(1024)S(1)}, f32[4096]{0:T(1024)S(1)}, f32[4096,2048]{1,0:T(8,128)}, /*index=5*/s32[]{:T(128)}, s32[]{:T(128)}, s32[]{:T(128)}, s32[]{:T(128)}) while((s32[]{:T(128)}, f32[2048]{0:T(1024)S(1)}, f32[2048]{0:T(1024)S(1)}, f32[4096]{0:T(1024)S(1)}, ...), condition=%wide.region_35.36_spmd.clone, body=%wide.region_32.35_spmd.clone.sunk | while | flops 7350279 | bytes 8503458 | solution.py:98
  517.6 13.0 %all-gather.2 = f32[16384]{0:T(1024)S(1)} all-gather(f32[2048]{0:T(1024)S(1)} %log_add_fusion.3), channel_id=4, replica_groups=mesh['row'=8,'col'=16] {'row'}, dimensions={0}, use_global_device_ids=true | all-gather | bytes 73728 | tf_op jit(solution)/shard_map/all_gather | solution.py:49
  530.7 45.3 %while.97 = (s32[]{:T(128)}, bf16[8,512,2048]{2,1,0:T(8,128)(2,1)}, s32[8]{0:T(128)S(1)}, f32[4096]{0:T(1024)S(1)}, f32[2048]{0:T(1024)S(1)}, /*index=5*/f32[409...) while((s32[]{:T(128)}, bf16[8,512,2048]{2,1,0:T(8,128)(2,1)}, s32[8]{0:T(128)S(1)}, ...), condition=%wide.region_39.40_spmd, body=%wide.region_38.39_spmd.sunk | while | flops 4194310 | bytes 6306471 | solution.py:111
  532.0 4.3 fusion.41
  537.7 4.3 fusion.41
  543.3 4.4 fusion.41
  549.0 4.3 fusion.41
  554.6 4.4 fusion.41
  560.3 4.3 fusion.41
  566.0 4.4 fusion.41
  571.7 4.3 fusion.41
  576.0 8.5 %convert_reduce_fusion = (f32[2048]{0:T(1024)S(1)}, f32[8,512]{1,0:T(8,128)S(1)}) fusion(bf16[8,512,2048]{2,1,0:T(8,128)(2,1)} %get-tuple-element.425), kind=kLoop, calls=%fused_computation.30 | loop fusion | flops 25159680 | bytes 16801792 | tf_op jit(solution)/shard_map/reduce_sum | solution.py:113
  586.7 6.0 fusion.15
  592.8 11.7 %fusion.11 = f32[4096,128]{1,0:T(8,128)} fusion(bf16[4096,2048]{1,0:T(8,128)(2,1)} %bitcast.82, bf16[2048,128]{1,0:T(8,128)(2,1)S(1)} %bitcast_dynamic-update-slice_fusion, bf16[4096,128]{1,0:T(8,128)(2,1)S(1)} %copy-done.1, f32[4096]{0:T(1024)S(1)} %bitcast.91), kind=kOutput, calls=%fused_computation.34 | convolution fusion | flops 2149580800 | bytes 20463616 | tf_op jit(solution)/shard_map/dot_general | solution.py:119
  604.5 18.1 %reduce-scatter.5.cloned.1.call-done = f32[256,128]{1,0:T(8,128)} async-done(((f32[2048,128]{1,0:T(8,128)}), f32[256,128]{1,0:T(8,128)}) %reduce-scatter.5.cloned.1.call-update) | async-done | bytes 131088 | tf_op jit(solution)/shard_map/reduce_scatter | solution.py:129
  622.6 77.2 %reduce-scatter.3.cloned.1.call-done = f32[256,128]{1,0:T(8,128)} async-done(((f32[4096,128]{1,0:T(8,128)}), f32[256,128]{1,0:T(8,128)}) %reduce-scatter.3.cloned.1.call-update) | async-done | bytes 131088 | tf_op jit(solution)/shard_map/reduce_scatter | solution.py:120
  (364 shorter events, 318.3 us)
Async XLA Ops:
  7.2 48.4 %all-gather.8.cloned.1.call-start = ((), (), s32[]{:S(2)}) async-start(), calls=%async_computation.2 | async-start | bytes 1114112 | tf_op jit(solution)/shard_map/all_gather | solution.py:56
  7.2 5.1 collective-permute-start
  7.2 5.2 collective-permute-start.1
  10.2 612.4 %reduce-scatter.5.cloned.1.call-start = ((), (), s32[]{:S(2)}) async-start(), calls=%async_computation.4 | async-start | bytes 1179648 | tf_op jit(solution)/shard_map/reduce_scatter | solution.py:129
  12.3 4.9 collective-permute-start.2
  12.4 4.8 collective-permute-start.3
  17.2 4.9 collective-permute-start.4
  17.2 4.9 collective-permute-start.5
  22.1 4.9 collective-permute-start.6
  105.0 81.7 %copy-start.2 = (f32[4096]{0:T(1024)S(1)}, f32[4096]{0:T(1024)}, u32[]{:S(2)}) copy-start(f32[4096]{0:T(1024)} %param.20) | copy-start | bytes 49156
  186.8 60.7 %copy-start.3 = (f32[2048]{0:T(1024)S(1)}, f32[2048]{0:T(1024)}, u32[]{:S(2)}) copy-start(f32[2048]{0:T(1024)} %param.21) | copy-start | bytes 24580
  530.7 53.8 %copy-start.1 = (bf16[4096,128]{1,0:T(8,128)(2,1)S(1)}, bf16[4096,128]{1,0:T(8,128)(2,1)}, u32[]{:S(2)}) copy-start(bf16[4096,128]{1,0:T(8,128)(2,1)} %all-gather.8.cloned.1.call-done) | copy-start | bytes 3145732
  576.0 10.7 %copy-start = (bf16[8,512,2048]{2,1,0:T(8,128)(2,1)S(1)}, bf16[8,512,2048]{2,1,0:T(8,128)(2,1)}, u32[]{:S(2)}) copy-start(bf16[8,512,2048]{2,1,0:T(8,128)(2,1)} %get-tuple-element.425) | copy-start | bytes 50331652
  592.7 107.0 %reduce-scatter.3.cloned.1.call-start = ((), (), s32[]{:S(2)}) async-start(), calls=%async_computation.3 | async-start | bytes 2228224 | tf_op jit(solution)/shard_map/reduce_scatter | solution.py:120
Sparse Core Ops, SparseCore 0:
  10.3 45.1 all-gather.7
  592.9 29.6 reduce-scatter.4
  626.4 73.2 reduce-scatter.2
